TPU v7x, 32 devices: a whole 2x2x4 slice. The times are simulated.
32 devices in a mesh: groups: 2 (over y), tile: 4 (over z), chan: 2 (over x), tm: 2 (over core).
Axes of the slice: x: 2, y: 2, z: 4, core: 2. Of those that a mesh axis runs over, the one named last changes fastest.
Arguments:
- latents: bfloat16 [8, 32, 576], P('tm', 'groups', 'tile'), parts along dimension 1, may hold values from -6 to 6
- tile_order: int32 [8], P('groups'), parts along dimension 0, may hold values from 0 to 3, each once
- w_in: bfloat16 [27, 16, 512], P(None, None, 'chan'), may hold values from -0.3125 to 0.3125
- gain_in: float32 [512], P('chan'), may hold values from 0.25 to 1.75
- shift_in: float32 [512], P('chan'), may hold values from -3 to 3
- w_mid: bfloat16 [27, 512, 512], P(None, None, 'chan'), may hold values from -0.0546875 to 0.0546875
- gain_mid: float32 [512], P('chan'), may hold values from 0.25 to 1.75
- shift_mid: float32 [512], P('chan'), may hold values from -3 to 3
- w_out: bfloat16 [3, 512], P(None, 'chan'), may hold values from -0.25 to 0.25
- blend_weight: float32 [8, 256], P('groups'), parts along dimension 0, may hold values from 0.25 to 4
Outputs:
- decoded: float32 [8, 6, 576], P('tm', 'groups', 'tile'), parts along dimension 1
There are 2 independent parts, one for each index of `groups`. A program takes and returns all parts, laid end to end along the dimension named above; an argument that names none is the same for every part. Nothing has to cross between parts.
Inputs may be any that keep to these rules, and one draw needn't show every extreme that they name: `tile_order`: each image block is held by exactly one latent block.
All inputs are finite; a program needn't handle non-finite values.
Results may differ from a plain program's by a relative error of at most 0.0037.
Values may be sent and summed in bfloat16 or wider, within the bound.
A program may use at most 64 MiB of HBM per device.

v0:
```python
import jax
import jax.numpy as jnp
from jax import lax
from jax.sharding import PartitionSpec as P

CH = 512
GROUPS = 32
TSIDE = 16
STRIDE = 12
GRID_X = 4
EPSILON = 1e-06


def shifted(value, axis, steps):
    count = lax.axis_size(axis)
    leading, last = (max(0, -steps), min(count, count - steps))
    return lax.ppermute(value, axis, [(source, source + steps) for source in range(leading, last)])


def window_index(tile_id, tiles):
    slots = jnp.arange(TSIDE * TSIDE, dtype=jnp.int32)
    row = tile_id // GRID_X * STRIDE + slots // TSIDE
    col = tile_id % GRID_X * STRIDE + slots % TSIDE
    valid = (row < tiles // GRID_X * STRIDE) & (col < GRID_X * STRIDE)
    block = row // STRIDE * GRID_X + col // STRIDE
    index = block * (STRIDE * STRIDE) + row % STRIDE * STRIDE + col % STRIDE
    return (jnp.where(valid, index, 0), valid)


def causal_conv(extended, weights, frames, side):
    pixels = side * side
    rows = jnp.arange(pixels, dtype=jnp.int32) // side
    cols = jnp.arange(pixels, dtype=jnp.int32) % side
    total = jnp.zeros((frames, weights.shape[2], pixels), jnp.float32)
    for depth in range(3):
        window = extended[depth : depth + frames]
        for down in range(3):
            for across in range(3):
                offset = (down - 1) * side + (across - 1)
                inside = (
                    (rows + down - 1 >= 0)
                    & (rows + down - 1 < side)
                    & (cols + across - 1 >= 0)
                    & (cols + across - 1 < side)
                )
                moved = jnp.roll(window, -offset, axis=2)
                moved = jnp.where(inside[None, None, :], moved, jnp.zeros_like(moved))
                total = total + jnp.einsum(
                    "fcp,co->fop",
                    moved,
                    weights[9 * depth + 3 * down + across],
                    preferred_element_type=jnp.float32,
                )
    return total


def with_history(values):
    frames = values.shape[0]
    earlier = shifted(values[frames - 2 :], "tm", 1)
    return jnp.concatenate([earlier, values], axis=0)


def normalize(values, gain, shift, total_frames):
    frames, chans, pixels = values.shape
    width = CH // GROUPS
    grouped = values.reshape(frames, chans // width, width, pixels)
    sums = jnp.sum(grouped, axis=(0, 2, 3))
    squares = jnp.sum(grouped * grouped, axis=(0, 2, 3))
    sums, squares = lax.psum((sums, squares), "tm")
    count = total_frames * width * pixels
    mean = sums / count
    variance = squares / count - mean * mean
    scale = lax.rsqrt(variance + EPSILON)
    normed = (grouped - mean[None, :, None, None]) * scale[None, :, None, None]
    normed = normed.reshape(frames, chans, pixels) * gain[None, :, None] + shift[None, :, None]
    return jax.nn.silu(normed).astype(jnp.bfloat16)


def spread(color, weight, index, total_pixels):
    numer = (
        jnp.zeros((color.shape[0], 3, total_pixels), jnp.float32)
        .at[:, :, index]
        .add(color * weight[None, None, :])
    )
    denom = jnp.zeros((total_pixels,), jnp.float32).at[index].add(weight)
    return (numer, denom)


def route_owned(numer, denom, tile_id, own):
    frames = numer.shape[0]
    margin = (GRID_X + 1) * own
    numer_wide = jnp.concatenate([numer, jnp.zeros((frames, 3, margin), jnp.float32)], axis=2)
    denom_wide = jnp.concatenate([denom, jnp.zeros((margin,), jnp.float32)], axis=0)
    first_pixel = tile_id * own

    def block_at(offset):
        start_pixel = first_pixel + offset * own
        return (
            lax.dynamic_slice_in_dim(numer_wide, start_pixel, own, 2),
            lax.dynamic_slice_in_dim(denom_wide, start_pixel, own, 0),
        )

    owned_numer, owned_denom = block_at(0)
    for offset in (1, GRID_X, GRID_X + 1):
        piece_numer, piece_denom = block_at(offset)
        got_numer, got_denom = shifted((piece_numer, piece_denom), "tile", offset)
        owned_numer = owned_numer + got_numer
        owned_denom = owned_denom + got_denom
    return (owned_numer, owned_denom)


def body(
    latents, tile_order, w_in, gain_in, shift_in, w_mid, gain_mid, shift_mid, w_out, blend_weight
):
    frames = latents.shape[0]
    total_frames = frames * lax.axis_size("tm")
    tiles = tile_order.shape[0]
    own = STRIDE * STRIDE
    total_pixels = tiles * own
    tile_id = lax.axis_index("tile")
    index, valid = window_index(tile_id, tiles)
    whole = lax.all_gather(latents, "tile", axis=2, tiled=True)
    blocks = whole.reshape(frames, whole.shape[1], tiles, own)
    image = (
        jnp.zeros_like(blocks)
        .at[:, :, tile_order]
        .set(blocks)
        .reshape(frames, whole.shape[1], total_pixels)
    )
    window = jnp.where(
        valid[None, None, :], jnp.take(image, index, axis=2), jnp.zeros((), jnp.bfloat16)
    )
    first = causal_conv(with_history(window), w_in, frames, TSIDE)
    hidden = normalize(first, gain_in, shift_in, total_frames)
    second = causal_conv(
        lax.all_gather(with_history(hidden), "chan", axis=1, tiled=True), w_mid, frames, TSIDE
    )
    upper = normalize(second, gain_mid, shift_mid, total_frames)
    color = jnp.einsum("oc,fcp->fop", w_out, upper, preferred_element_type=jnp.float32)
    weight = jnp.where(valid, blend_weight[tile_id], jnp.float32(0.0))
    numer, denom = spread(color, weight, index, total_pixels)
    numer, denom = route_owned(numer, denom, tile_id, own)
    numer = lax.psum(numer, "chan")
    return numer / denom[None, None, :]


def solution(mesh):
    placed = (
        P("tm", "groups", "tile"),
        P("groups"),
        P(None, None, "chan"),
        P("chan"),
        P("chan"),
        P(None, None, "chan"),
        P("chan"),
        P("chan"),
        P(None, "chan"),
        P("groups", None),
    )
    return jax.shard_map(
        body, mesh=mesh, in_specs=placed, out_specs=P("tm", "groups", "tile"), check_vma=False
    )
```

profile of v0, /device:TPU:0, one launch (start us, length us, event | category | flops | bytes accessed | tf_op | source)
XLA Modules:
  0.0 141.7 jit_solution(11770328538480830236)
XLA Ops:
  6.6 1.0 copy.204
  7.6 18.3 %all_gather.6 = bf16[4,16,576]{1,0,2:T(4,128)(2,1)S(1)} all-gather(bf16[4,16,144]{1,0,2:T(4,128)(2,1)S(1)} %copy.204), channel_id=1, replica_groups=mesh['groups'=2,'tile'=4,'chan'=2,'tm'=2] {'tile'}, dimensions={2}, use_global_device_ids=true | all-gather | bytes 92160 | tf_op jit(solution)/shard_map/all_gather | solution.py:122
  27.9 1.0 gather_fusion
  29.1 1.3 collective-permute-start
  43.4 2.5 %all-reduce.3 = (f32[16]{0:T(128)S(1)}, f32[16]{0:T(128)S(1)}) all-reduce(f32[16]{0:T(128)S(1)} %reduce_sum.54, f32[16]{0:T(128)S(1)} %reduce_sum.51), channel_id=1, replica_groups=mesh['groups'=2,'tile'=4,'chan'=2,'tm'=2] {'tm'}, use_global_device_ids=true, to_apply=%region_6.7 | all-reduce | flops 32 | bytes 256 | tf_op jit(solution)/shard_map/psum | solution.py:69
  46.6 2.3 %collective-permute-start.1 = (bf16[2,256,256]{1,2,0:T(8,128)(2,1)S(1)}, bf16[2,256,256]{1,2,0:T(8,128)(2,1)S(1)}, u32[]{:S(2)}, u32[]{:S(2)}) collective-permute-start(bf16[2,256,256]{1,2,0:T(8,128)(2,1)S(1)} %slice.825), channel_id=1, source_target_pairs={{0,1},{2,3},{4,5},{6,7},{8,9},{10,11},{12,13},{14,15},{16,17},{18,... | collective-permute-start | bytes 786440 | tf_op jit(solution)/shard_map/ppermute | solution.py:17
  48.9 1.1 collective-permute-done.1
  51.0 2.3 %scatter_custom_fusion.2 = f32[576]{0:T(1024)S(1)} fusion(s32[256]{0:T(256)S(1)} %bitcast.322, f32[256]{0:T(256)S(1)} %broadcast_select_fusion, f32[]{:T(128)} %constant.166.clone.1), kind=kCustom, calls=%fused_computation.579 | custom fusion | flops 256 | bytes 2308 | tf_op jit(solution)/shard_map/scatter-add | solution.py:85
  53.4 3.4 %collective-permute-start.5 = (f32[144]{0:T(256)S(1)}, f32[144]{0:T(256)S(1)}, u32[]{:S(2)}, u32[]{:S(2)}) collective-permute-start(f32[144]{0:T(256)S(1)} %get-tuple-element.115), channel_id=1, source_target_pairs={{0,4},{4,8},{8,12},{1,5},{5,9},{9,13},{2,6},{6,10},{10,14},{3,7},{... | collective-permute-start | bytes 1736 | tf_op jit(solution)/shard_map/ppermute | solution.py:17
  58.4 21.1 %all-gather.2.cloned.1.call-done = bf16[6,512,256]{1,2,0:T(8,128)(2,1)} async-done(((bf16[6,256,256]{1,2,0:T(8,128)(2,1)}), bf16[6,512,256]{1,2,0:T(8,128)(2,1)}) %all-gather.2.cloned.1.call-update) | async-done | bytes 1572880 | tf_op jit(solution)/shard_map/all_gather | solution.py:136
  79.5 4.2 %fusion.506 = (bf16[4,512,239]{1,2,0:T(8,128)(2,1)S(1)}, bf16[4,512,239]{1,2,0:T(8,128)(2,1)S(1)}, bf16[4,512,239]{1,2,0:T(8,128)(2,1)S(1)}, bf16[4,512,239]{1,2...) fusion(bf16[6,512,256]{1,2,0:T(8,128)(2,1)} %all-gather.2.cloned.1.call-done), kind=kLoop, calls=%fused_computation.741 | loop fusion | bytes 11747328 | tf_op jit(solution)/shard_map/jit(_roll_static)/slice | solution.py:46
  83.8 1.4 %fusion.23 = f32[4,256,256]{2,1,0:T(8,128)S(1)} fusion(bf16[4,512,239]{1,2,0:T(8,128)(2,1)S(1)} %get-tuple-element.30, bf16[4,512,17]{1,2,0:T(8,128)(2,1)S(1)} %get-tuple-element.36, pred[256]{0:T(512)(128)(4,1)S(1)} %and_and_fusion.8, bf16[27,512,256]{2,1,0:T(8,128)(2,1)} %param.15), kind=kOutput, calls=%fused_computation.84 | convolution fusion | flops 271056896 | bytes 2359552 | tf_op jit(solution)/shard_map/fcp,co->fop/dot_general | solution.py:48
  85.2 1.4 %convolution_bitcast_fusion.8 = f32[4,256,256]{1,2,0:T(8,128)S(1)} fusion(bf16[4,512,239]{1,2,0:T(8,128)(2,1)S(1)} %get-tuple-element.27, bf16[4,512,17]{1,2,0:T(8,128)(2,1)S(1)} %get-tuple-element.33, pred[256]{0:T(512)(128)(4,1)S(1)} %and_and_fusion.8, bf16[27,512,256]{2,1,0:T(8,128)(2,1)} %param.15), kind=kOutput, calls=%fused_computation.12 | convolution fusion | flops 271056896 | bytes 2359552 | tf_op jit(solution)/shard_map/fcp,co->fop/dot_general | solution.py:48
  87.4 1.4 %convolution_bitcast_fusion.7 = f32[4,256,256]{1,2,0:T(8,128)S(1)} fusion(bf16[4,512,240]{1,2,0:T(8,128)(2,1)S(1)} %get-tuple-element.39, bf16[4,512,16]{1,2,0:T(8,128)(2,1)S(1)} %get-tuple-element.45, pred[256]{0:T(512)(128)(4,1)S(1)} %get-tuple-element.131, bf16[27,512,256]{2,1,0:T(8,128)(2,1)} %param.15), kind=kOutput, calls=%fused_computation.11 | convolution fusion | flops 271056896 | bytes 2359552 | tf_op jit(solution)/shard_map/fcp,co->fop/dot_general | solution.py:48
  89.6 1.5 %convolution_bitcast_fusion.6 = f32[4,256,256]{1,2,0:T(8,128)S(1)} fusion(bf16[4,512,241]{1,2,0:T(8,128)(2,1)S(1)} %get-tuple-element.51, bf16[4,512,15]{1,2,0:T(8,128)(2,1)S(1)} %get-tuple-element.57, pred[256]{0:T(512)(128)(4,1)S(1)} %get-tuple-element.130, bf16[27,512,256]{2,1,0:T(8,128)(2,1)} %param.15), kind=kOutput, calls=%fused_computation.10 | convolution fusion | flops 271056896 | bytes 2359552 | tf_op jit(solution)/shard_map/fcp,co->fop/dot_general | solution.py:48
  91.9 1.4 %convolution_bitcast_fusion.5 = f32[4,256,256]{1,2,0:T(8,128)S(1)} fusion(bf16[4,512,255]{1,2,0:T(8,128)(2,1)S(1)} %get-tuple-element.14, bf16[4,512,1]{1,2,0:T(2,128)(2,1)S(1)} %get-tuple-element.20, pred[256]{0:T(512)(128)(4,1)S(1)} %get-tuple-element.129, bf16[27,512,256]{2,1,0:T(8,128)(2,1)} %param.15), kind=kOutput, calls=%fused_computation.9 | convolution fusion | flops 271056896 | bytes 2359552 | tf_op jit(solution)/shard_map/fcp,co->fop/dot_general | solution.py:48
  93.4 1.6 %convolution_bitcast_fusion.2 = f32[4,256,256]{1,2,0:T(8,128)S(1)} fusion(bf16[4,512,15]{1,2,0:T(8,128)(2,1)S(1)} %get-tuple-element.56, bf16[4,512,241]{1,2,0:T(8,128)(2,1)S(1)} %get-tuple-element.50, pred[256]{0:T(512)(128)(4,1)S(1)} %get-tuple-element.126, bf16[27,512,256]{2,1,0:T(8,128)(2,1)} %param.15), kind=kOutput, calls=%fused_computation.6 | convolution fusion | flops 271056896 | bytes 2359552 | tf_op jit(solution)/shard_map/fcp,co->fop/dot_general | solution.py:48
  95.0 1.4 %convolution_bitcast_fusion.1 = f32[4,256,256]{1,2,0:T(8,128)S(1)} fusion(bf16[4,512,16]{1,2,0:T(8,128)(2,1)S(1)} %get-tuple-element.44, bf16[4,512,240]{1,2,0:T(8,128)(2,1)S(1)} %get-tuple-element.38, pred[256]{0:T(512)(128)(4,1)S(1)} %get-tuple-element.125, bf16[27,512,256]{2,1,0:T(8,128)(2,1)} %param.15), kind=kOutput, calls=%fused_computation.5 | convolution fusion | flops 271056896 | bytes 2359552 | tf_op jit(solution)/shard_map/fcp,co->fop/dot_general | solution.py:48
  96.4 1.6 %convolution_bitcast_fusion = f32[4,256,256]{1,2,0:T(8,128)S(1)} fusion(bf16[4,512,17]{1,2,0:T(8,128)(2,1)S(1)} %get-tuple-element.32, bf16[4,512,239]{1,2,0:T(8,128)(2,1)S(1)} %get-tuple-element.26, pred[256]{0:T(512)(128)(4,1)S(1)} %get-tuple-element.124, bf16[27,512,256]{2,1,0:T(8,128)(2,1)} %param.15), kind=kOutput, calls=%fused_computation.4 | convolution fusion | flops 271056896 | bytes 2359552 | tf_op jit(solution)/shard_map/fcp,co->fop/dot_general | solution.py:48
  98.0 1.5 %convolution_add_fusion.31 = f32[4,256,256]{2,1,0:T(8,128)S(1)} fusion(f32[4,256,256]{2,1,0:T(8,128)S(1)} %fusion.23, bf16[4,512,240]{1,2,0:T(8,128)(2,1)S(1)} %get-tuple-element.42, bf16[4,512,16]{1,2,0:T(8,128)(2,1)S(1)} %get-tuple-element.48, pred[256]{0:T(512)(128)(4,1)S(1)} %get-tuple-element.131, bf16[27,512,256]{2,1,0:T(8,128)(2,1)} %param.15), kind=kOutput, calls=%fused_computation.77 | convolution fusion | flops 271319040 | bytes 3408128 | tf_op jit(solution)/shard_map/fcp,co->fop/dot_general | solution.py:48
  109.4 2.5 %all-reduce.2 = (f32[16]{0:T(128)S(1)}, f32[16]{0:T(128)S(1)}) all-reduce(f32[16]{0:T(128)S(1)} %reduce_sum.75, f32[16]{0:T(128)S(1)} %reduce_sum.72), channel_id=1, replica_groups=mesh['groups'=2,'tile'=4,'chan'=2,'tm'=2] {'tm'}, use_global_device_ids=true, to_apply=%region_12.13 | all-reduce | flops 32 | bytes 256 | tf_op jit(solution)/shard_map/psum | solution.py:69
  113.1 8.5 %scatter_fusion.1 = f32[4,3,576]{1,0,2:T(4,128)S(1)} fusion(f32[4,3,576]{1,0,2:T(4,128)S(1)} %broadcast_in_dim.385, s32[256]{0:T(256)S(1)} %bitcast.323, f32[256,4,3]{2,1,0:T(4,128)S(1)} %copy.210), kind=kCustom, calls=%fused_computation.2 | custom fusion | flops 3072 | bytes 37888 | tf_op jit(solution)/shard_map/scatter-add | solution.py:83
  122.2 3.4 %collective-permute-start.2 = (f32[4,3,144]{2,0,1:T(4,128)S(1)}, f32[4,3,144]{2,0,1:T(4,128)S(1)}, u32[]{:S(2)}, u32[]{:S(2)}) collective-permute-start(f32[4,3,144]{2,0,1:T(4,128)S(1)} %get-tuple-element.112), channel_id=1, source_target_pairs={{0,4},{4,8},{8,12},{1,5},{5,9},{9,13},{2,6},{6,10},{10,14},{3,7},{... | collective-permute-start | bytes 20744 | tf_op jit(solution)/shard_map/ppermute | solution.py:17
  127.1 7.1 %psum.39 = f32[4,3,144]{2,0,1:T(4,128)S(1)} all-reduce(f32[4,3,144]{2,0,1:T(4,128)S(1)} %fusion.326), channel_id=1, replica_groups=mesh['groups'=2,'tile'=4,'chan'=2,'tm'=2] {'chan'}, use_global_device_ids=true, to_apply=%region_14.15 | all-reduce | flops 1728 | bytes 13824 | tf_op jit(solution)/shard_map/psum | solution.py:143
  (144 shorter events, 34.2 us)
Async XLA Ops:
  6.5 44.4 %copy-start = (f32[4,256]{1,0:T(4,128)S(1)}, f32[4,256]{1,0:T(4,128)}, u32[]{:S(2)}) copy-start(f32[4,256]{1,0:T(4,128)} %param.19) | copy-start | bytes 12292
  6.5 24.9 %copy-start.3 = (bf16[27,16,256]{2,1,0:T(8,128)(2,1)S(1)}, bf16[27,16,256]{2,1,0:T(8,128)(2,1)}, u32[]{:S(2)}) copy-start(bf16[27,16,256]{2,1,0:T(8,128)(2,1)} %param.12) | copy-start | bytes 663556
  6.5 72.9 %all-gather.2.cloned.1.call-start = ((), (), s32[]{:S(2)}) async-start(), calls=%async_computation | async-start | bytes 2359296 | tf_op jit(solution)/shard_map/all_gather | solution.py:136
  29.1 2.1 %collective-permute-start = (bf16[2,16,256]{2,1,0:T(8,128)(2,1)S(1)}, bf16[2,16,256]{2,1,0:T(8,128)(2,1)S(1)}, u32[]{:S(2)}, u32[]{:S(2)}) collective-permute-start(bf16[2,16,256]{2,1,0:T(8,128)(2,1)S(1)} %slice.742), channel_id=1, source_target_pairs={{0,1},{2,3},{4,5},{6,7},{8,9},{10,11},{12,13},{14,15},{16,17},{18,... | collective-permute-start | bytes 49160 | tf_op jit(solution)/shard_map/ppermute | solution.py:17
  42.2 4.1 %copy-start.4 = (f32[256]{0:T(256)S(1)}, f32[256]{0:T(256)}, u32[]{:S(2)}) copy-start(f32[256]{0:T(256)} %param.14) | copy-start | bytes 3076
  42.2 4.0 %copy-start.5 = (f32[256]{0:T(256)S(1)}, f32[256]{0:T(256)}, u32[]{:S(2)}) copy-start(f32[256]{0:T(256)} %param.13) | copy-start | bytes 3076
  46.6 3.4 %collective-permute-start.1 = (bf16[2,256,256]{1,2,0:T(8,128)(2,1)S(1)}, bf16[2,256,256]{1,2,0:T(8,128)(2,1)S(1)}, u32[]{:S(2)}, u32[]{:S(2)}) collective-permute-start(bf16[2,256,256]{1,2,0:T(8,128)(2,1)S(1)} %slice.825), channel_id=1, source_target_pairs={{0,1},{2,3},{4,5},{6,7},{8,9},{10,11},{12,13},{14,15},{16,17},{18,... | collective-permute-start | bytes 786440 | tf_op jit(solution)/shard_map/ppermute | solution.py:17
  53.4 72.8 %collective-permute-start.5 = (f32[144]{0:T(256)S(1)}, f32[144]{0:T(256)S(1)}, u32[]{:S(2)}, u32[]{:S(2)}) collective-permute-start(f32[144]{0:T(256)S(1)} %get-tuple-element.115), channel_id=1, source_target_pairs={{0,4},{4,8},{8,12},{1,5},{5,9},{9,13},{2,6},{6,10},{10,14},{3,7},{... | collective-permute-start | bytes 1736 | tf_op jit(solution)/shard_map/ppermute | solution.py:17
  56.9 70.0 %collective-permute-start.6 = (f32[144]{0:T(256)S(1)}, f32[144]{0:T(256)S(1)}, u32[]{:S(2)}, u32[]{:S(2)}) collective-permute-start(f32[144]{0:T(256)S(1)} %get-tuple-element.116), channel_id=1, source_target_pairs={} | collective-permute-start | bytes 1736 | tf_op jit(solution)/shard_map/ppermute | solution.py:17
  57.5 69.4 %collective-permute-start.7 = (f32[144]{0:T(256)S(1)}, f32[144]{0:T(256)S(1)}, u32[]{:S(2)}, u32[]{:S(2)}) collective-permute-start(f32[144]{0:T(256)S(1)} %get-tuple-element.117), channel_id=1, source_target_pairs={} | collective-permute-start | bytes 1736 | tf_op jit(solution)/shard_map/ppermute | solution.py:17
  79.5 4.2 %copy-start.2 = (bf16[6,512,256]{1,2,0:T(8,128)(2,1)S(1)}, bf16[6,512,256]{1,2,0:T(8,128)(2,1)}, u32[]{:S(2)}) copy-start(bf16[6,512,256]{1,2,0:T(8,128)(2,1)} %all-gather.2.cloned.1.call-done) | copy-start | bytes 4718596
  93.4 6.1 %slice-start = ((s8[7077888]{0:T(1024)(128)(4,1)}), s8[4194304]{0:T(1024)(128)(4,1)S(1)}, s32[]{:S(2)}) async-start(s8[7077888]{0:T(1024)(128)(4,1)} %bitcast.319), calls=%async_computation.1 | async-start | bytes 8388608
  96.4 3.1 %slice-start.1 = ((s8[7077888]{0:T(1024)(128)(4,1)}), s8[2883584]{0:T(1024)(128)(4,1)S(1)}, s32[]{:S(2)}) async-start(s8[7077888]{0:T(1024)(128)(4,1)} %bitcast.319), calls=%async_computation.2 | async-start | bytes 5767168
  108.4 3.8 %copy-start.6 = (bf16[3,256]{1,0:T(4,128)(2,1)S(1)}, bf16[3,256]{1,0:T(4,128)(2,1)}, u32[]{:S(2)}) copy-start(bf16[3,256]{1,0:T(4,128)(2,1)} %param.18) | copy-start | bytes 4612
  108.4 3.8 %copy-start.7 = (f32[256]{0:T(256)S(1)}, f32[256]{0:T(256)}, u32[]{:S(2)}) copy-start(f32[256]{0:T(256)} %param.17) | copy-start | bytes 3076
  108.4 3.8 %copy-start.8 = (f32[256]{0:T(256)S(1)}, f32[256]{0:T(256)}, u32[]{:S(2)}) copy-start(f32[256]{0:T(256)} %param.16) | copy-start | bytes 3076
  112.7 22.2 %copy-start.1 = (f32[4,256]{1,0:T(4,128)S(1)}, f32[4,256]{1,0:T(4,128)}, u32[]{:S(2)}) copy-start(f32[4,256]{1,0:T(4,128)} %param.19) | copy-start | bytes 12292
  122.2 4.8 %collective-permute-start.2 = (f32[4,3,144]{2,0,1:T(4,128)S(1)}, f32[4,3,144]{2,0,1:T(4,128)S(1)}, u32[]{:S(2)}, u32[]{:S(2)}) collective-permute-start(f32[4,3,144]{2,0,1:T(4,128)S(1)} %get-tuple-element.112), channel_id=1, source_target_pairs={{0,4},{4,8},{8,12},{1,5},{5,9},{9,13},{2,6},{6,10},{10,14},{3,7},{... | collective-permute-start | bytes 20744 | tf_op jit(solution)/shard_map/ppermute | solution.py:17
  125.6 1.4 %collective-permute-start.3 = (f32[4,3,144]{2,0,1:T(4,128)S(1)}, f32[4,3,144]{2,0,1:T(4,128)S(1)}, u32[]{:S(2)}, u32[]{:S(2)}) collective-permute-start(f32[4,3,144]{2,0,1:T(4,128)S(1)} %get-tuple-element.113), channel_id=1, source_target_pairs={} | collective-permute-start | bytes 20744 | tf_op jit(solution)/shard_map/ppermute | solution.py:17
  126.2 0.8 collective-permute-start.4
Sparse Core Ops, SparseCore 0:
  51.1 28.3 all-gather.1
where the time goes:
time: 142 us
  matrix products  33.9 us (24%)
  blocking collectives  30.3 us (21%)
  waiting for transfers between devices  23 us (16%)
  other arithmetic  14.9 us (10%)
  between operations  14.3 us (10%)
  starting transfers between devices  13.2 us (9%)
  local copies, waits for them, and re-layouts  12.1 us (9%)
    dot_general x54, matrix products, causal_conv(): jnp.einsum('fcp,co->fop', moved, weights[9 * depth + 3 * down + across],...  33.5 us
    all_gather x1, waiting for transfers between devices, body(): lax.all_gather(with_history(hidden), 'chan', axis=1, tiled=True)  21.1 us
    all_gather x1, blocking collectives, body(): whole = lax.all_gather(latents, 'tile', axis=2, tiled=True)  18.3 us
    ppermute x8, starting transfers between devices, shifted(): lax.ppermute(value, axis, [(source, source + steps) for source in range(l...  13.2 us
    scatter-add x1, other arithmetic, spread(): numer = jnp.zeros((color.shape[0], 3, total_pixels), jnp.float32).at[:, :...  8.52 us
    psum x1, blocking collectives, body(): numer = lax.psum(numer, 'chan')  7.13 us
    slice x8, local copies, waits for them, and re-layouts, causal_conv(): moved = jnp.roll(window, -offset, axis=2)  6.55 us
    psum x2, blocking collectives, normalize(): sums, squares = lax.psum((sums, squares), 'tm')  4.95 us
  transfers between devices with their start and end apart: 9, of which 3 were waited for; matrix products, arithmetic and copies ran while one was open for 30% of the time, Pallas kernels for 0%

commit v1 on v0

--- a/solution.py
+++ b/solution.py
@@ -9,6 +9,25 @@
 STRIDE = 12
 GRID_X = 4
 EPSILON = 1e-06
+
+
+def gather_around(array, axis, dim):
+    size, here, rows = (lax.axis_size(axis), lax.axis_index(axis), array.shape[dim])
+    right = [(i, (i + 1) % size) for i in range(size)]
+    behind = [(i, (i - 1) % size) for i in range(size)]
+    out = jnp.zeros((*array.shape[:dim], size * rows, *array.shape[dim + 1 :]), array.dtype)
+    out = lax.dynamic_update_slice_in_dim(out, array, here * rows, axis=dim)
+    from_left = from_right = array
+    half = size // 2
+    for turn in range(1, half + 1):
+        from_left = lax.ppermute(from_left, axis, right)
+        out = lax.dynamic_update_slice_in_dim(out, from_left, (here - turn) % size * rows, axis=dim)
+        if turn < size - half:
+            from_right = lax.ppermute(from_right, axis, behind)
+            out = lax.dynamic_update_slice_in_dim(
+                out, from_right, (here + turn) % size * rows, axis=dim
+            )
+    return out
 
 
 def shifted(value, axis, steps):
@@ -119,7 +138,7 @@
     total_pixels = tiles * own
     tile_id = lax.axis_index("tile")
     index, valid = window_index(tile_id, tiles)
-    whole = lax.all_gather(latents, "tile", axis=2, tiled=True)
+    whole = gather_around(latents, "tile", 2)
     blocks = whole.reshape(frames, whole.shape[1], tiles, own)
     image = (
         jnp.zeros_like(blocks)

time: 142 us -> 134 us (0.944)
  blocking collectives: 30.3 us -> 12.1 us
  waiting for transfers between devices: 23 us -> 27.2 us
  starting transfers between devices: 13.2 us -> 16.2 us
  local copies, waits for them, and re-layouts: 12.1 us -> 14.5 us
    all_gather x1 -> x0, blocking collectives: 18.3 us -> none  [body(): whole = lax.all_gather(latents, 'tile', axis=2, tiled=True)]
    ppermute x0 -> x3, starting transfers between devices: none -> 5.14 us  [the longest x2 3.05 us: gather_around(): from_left = lax.ppermute(from_left, axis, right)]
    ppermute x0 -> x3, waiting for transfers between devices: none -> 4.26 us  [the longest x2 4.26 us: gather_around(): from_left = lax.ppermute(from_left, axis, right)]
    dynamic_update_slice x0 -> x4, local copies, waits for them, and re-layouts: none -> 3.43 us  [the longest x2 1.56 us: gather_around(): lax.dynamic_update_slice_in_dim(out, from_left, (here - turn) % size * ro...]
    ppermute x8, starting transfers between devices: 13.2 us -> 11 us  [shifted(): lax.ppermute(value, axis, [(source, source + steps) for source in range(l...]
  transfers between devices with their start and end apart: 9 -> 12, of which waited for: 3 -> 5; matrix products, arithmetic and copies ran while one was open for 30% -> 35% of each run, Pallas kernels for 0% -> 0%
where the time goes in v1:
time: 134 us; the launch traced here: 133 us
  matrix products  33.9 us (25%)
  waiting for transfers between devices  27.2 us (20%)
  starting transfers between devices  16.2 us (12%)
  other arithmetic  14.9 us (11%)
  local copies, waits for them, and re-layouts  14.5 us (11%)
  between operations  14.4 us (11%)
  blocking collectives  12.1 us (9%)
    dot_general x54, matrix products, causal_conv(): jnp.einsum('fcp,co->fop', moved, weights[9 * depth + 3 * down + across],...  33.4 us
    all_gather x1, waiting for transfers between devices, body(): lax.all_gather(with_history(hidden), 'chan', axis=1, tiled=True)  21 us
    ppermute x8, starting transfers between devices, shifted(): lax.ppermute(value, axis, [(source, source + steps) for source in range(l...  11 us
    scatter-add x1, other arithmetic, spread(): numer = jnp.zeros((color.shape[0], 3, total_pixels), jnp.float32).at[:, :...  8.52 us
    psum x1, blocking collectives, body(): numer = lax.psum(numer, 'chan')  7.14 us
    slice x8, local copies, waits for them, and re-layouts, causal_conv(): moved = jnp.roll(window, -offset, axis=2)  6.7 us
    psum x2, blocking collectives, normalize(): sums, squares = lax.psum((sums, squares), 'tm')  4.96 us
    ppermute x2, waiting for transfers between devices, gather_around(): from_left = lax.ppermute(from_left, axis, right)  4.26 us
  transfers between devices with their start and end apart: 12, of which 5 were waited for; matrix products, arithmetic and copies ran while one was open for 35% of the time, Pallas kernels for 0%

profile of v1, /device:TPU:0, one launch (start us, length us, event | category | flops | bytes accessed | tf_op | source)
XLA Modules:
  0.0 133.1 jit_solution(11375420098898952887)
XLA Ops:
  6.5 3.1 %collective-permute-start = (bf16[4,16,144]{2,1,0:T(8,128)(2,1)}, bf16[4,16,144]{2,1,0:T(8,128)(2,1)S(1)}, u32[]{:S(2)}, u32[]{:S(2)}) collective-permute-start(bf16[4,16,144]{2,1,0:T(8,128)(2,1)} %param.10), channel_id=1, source_target_pairs={{0,4},{4,8},{8,12},{12,0},{1,5},{5,9},{9,13},{13,1},{2,6},{6,10},{... | collective-permute-start | bytes 55304 | tf_op jit(solution)/shard_map/ppermute | solution.py:23
  9.6 2.1 %collective-permute-start.1 = (bf16[4,16,144]{2,1,0:T(8,128)(2,1)}, bf16[4,16,144]{2,1,0:T(8,128)(2,1)S(1)}, u32[]{:S(2)}, u32[]{:S(2)}) collective-permute-start(bf16[4,16,144]{2,1,0:T(8,128)(2,1)} %param.10), channel_id=1, source_target_pairs={{0,12},{4,0},{8,4},{12,8},{1,13},{5,1},{9,5},{13,9},{2,14},{6,2},{... | collective-permute-start | bytes 55304 | tf_op jit(solution)/shard_map/ppermute | solution.py:26
  12.5 1.4 %collective-permute-done = bf16[4,16,144]{2,1,0:T(8,128)(2,1)S(1)} collective-permute-done((bf16[4,16,144]{2,1,0:T(8,128)(2,1)}, bf16[4,16,144]{2,1,0:T(8,128)(2,1)S(1)}, u32[]{:S(2)}, u32[]{:S(2)}) %collective-permute-start) | collective-permute-done | bytes 18464 | tf_op jit(solution)/shard_map/ppermute | solution.py:23
  16.7 2.9 %collective-permute-done.2 = bf16[4,16,144]{2,1,0:T(8,128)(2,1)S(1)} collective-permute-done((bf16[4,16,144]{2,1,0:T(8,128)(2,1)S(1)}, bf16[4,16,144]{2,1,0:T(8,128)(2,1)S(1)}, u32[]{:S(2)}, u32[]{:S(2)}) %collective-permute-start.2) | collective-permute-done | bytes 18464 | tf_op jit(solution)/shard_map/ppermute | solution.py:23
  22.7 1.3 collective-permute-start.3
  37.0 2.5 %all-reduce.3 = (f32[16]{0:T(128)S(1)}, f32[16]{0:T(128)S(1)}) all-reduce(f32[16]{0:T(128)S(1)} %reduce_sum.54, f32[16]{0:T(128)S(1)} %reduce_sum.51), channel_id=1, replica_groups=mesh['groups'=2,'tile'=4,'chan'=2,'tm'=2] {'tm'}, use_global_device_ids=true, to_apply=%region_6.7 | all-reduce | flops 32 | bytes 256 | tf_op jit(solution)/shard_map/psum | solution.py:88
  40.2 2.3 %collective-permute-start.4 = (bf16[2,256,256]{1,2,0:T(8,128)(2,1)S(1)}, bf16[2,256,256]{1,2,0:T(8,128)(2,1)S(1)}, u32[]{:S(2)}, u32[]{:S(2)}) collective-permute-start(bf16[2,256,256]{1,2,0:T(8,128)(2,1)S(1)} %slice.825), channel_id=1, source_target_pairs={{0,1},{2,3},{4,5},{6,7},{8,9},{10,11},{12,13},{14,15},{16,17},{18,... | collective-permute-start | bytes 786440 | tf_op jit(solution)/shard_map/ppermute | solution.py:36
  44.6 2.3 %scatter_custom_fusion.2 = f32[576]{0:T(1024)S(1)} fusion(s32[256]{0:T(256)S(1)} %bitcast.320, f32[256]{0:T(256)S(1)} %broadcast_select_fusion, f32[]{:T(128)} %constant.183.clone.1), kind=kCustom, calls=%fused_computation.579 | custom fusion | flops 256 | bytes 2308 | tf_op jit(solution)/shard_map/scatter-add | solution.py:104
  47.7 1.3 collective-permute-start.8
  49.8 21.0 %all-gather.2.cloned.1.call-done = bf16[6,512,256]{1,2,0:T(8,128)(2,1)} async-done(((bf16[6,256,256]{1,2,0:T(8,128)(2,1)}), bf16[6,512,256]{1,2,0:T(8,128)(2,1)}) %all-gather.2.cloned.1.call-update) | async-done | bytes 1572880 | tf_op jit(solution)/shard_map/all_gather | solution.py:155
  70.8 4.4 %fusion.506 = (bf16[4,512,239]{1,2,0:T(8,128)(2,1)S(1)}, bf16[4,512,239]{1,2,0:T(8,128)(2,1)S(1)}, bf16[4,512,239]{1,2,0:T(8,128)(2,1)S(1)}, bf16[4,512,239]{1,2...) fusion(bf16[6,512,256]{1,2,0:T(8,128)(2,1)} %all-gather.2.cloned.1.call-done), kind=kLoop, calls=%fused_computation.741 | loop fusion | bytes 11747328 | tf_op jit(solution)/shard_map/jit(_roll_static)/slice | solution.py:65
  75.2 1.4 %fusion.23 = f32[4,256,256]{2,1,0:T(8,128)S(1)} fusion(bf16[4,512,239]{1,2,0:T(8,128)(2,1)S(1)} %get-tuple-element.30, bf16[4,512,17]{1,2,0:T(8,128)(2,1)S(1)} %get-tuple-element.36, pred[256]{0:T(512)(128)(4,1)S(1)} %and_and_fusion.8, bf16[27,512,256]{2,1,0:T(8,128)(2,1)} %param.15), kind=kOutput, calls=%fused_computation.84 | convolution fusion | flops 271056896 | bytes 2359552 | tf_op jit(solution)/shard_map/fcp,co->fop/dot_general | solution.py:67
  76.7 1.4 %convolution_bitcast_fusion.8 = f32[4,256,256]{1,2,0:T(8,128)S(1)} fusion(bf16[4,512,239]{1,2,0:T(8,128)(2,1)S(1)} %get-tuple-element.27, bf16[4,512,17]{1,2,0:T(8,128)(2,1)S(1)} %get-tuple-element.33, pred[256]{0:T(512)(128)(4,1)S(1)} %and_and_fusion.8, bf16[27,512,256]{2,1,0:T(8,128)(2,1)} %param.15), kind=kOutput, calls=%fused_computation.12 | convolution fusion | flops 271056896 | bytes 2359552 | tf_op jit(solution)/shard_map/fcp,co->fop/dot_general | solution.py:67
  78.8 1.4 %convolution_bitcast_fusion.7 = f32[4,256,256]{1,2,0:T(8,128)S(1)} fusion(bf16[4,512,240]{1,2,0:T(8,128)(2,1)S(1)} %get-tuple-element.39, bf16[4,512,16]{1,2,0:T(8,128)(2,1)S(1)} %get-tuple-element.45, pred[256]{0:T(512)(128)(4,1)S(1)} %get-tuple-element.131, bf16[27,512,256]{2,1,0:T(8,128)(2,1)} %param.15), kind=kOutput, calls=%fused_computation.11 | convolution fusion | flops 271056896 | bytes 2359552 | tf_op jit(solution)/shard_map/fcp,co->fop/dot_general | solution.py:67
  81.0 1.4 %convolution_bitcast_fusion.6 = f32[4,256,256]{1,2,0:T(8,128)S(1)} fusion(bf16[4,512,241]{1,2,0:T(8,128)(2,1)S(1)} %get-tuple-element.51, bf16[4,512,15]{1,2,0:T(8,128)(2,1)S(1)} %get-tuple-element.57, pred[256]{0:T(512)(128)(4,1)S(1)} %get-tuple-element.130, bf16[27,512,256]{2,1,0:T(8,128)(2,1)} %param.15), kind=kOutput, calls=%fused_computation.10 | convolution fusion | flops 271056896 | bytes 2359552 | tf_op jit(solution)/shard_map/fcp,co->fop/dot_general | solution.py:67
  83.3 1.5 %convolution_bitcast_fusion.5 = f32[4,256,256]{1,2,0:T(8,128)S(1)} fusion(bf16[4,512,255]{1,2,0:T(8,128)(2,1)S(1)} %get-tuple-element.14, bf16[4,512,1]{1,2,0:T(2,128)(2,1)S(1)} %get-tuple-element.20, pred[256]{0:T(512)(128)(4,1)S(1)} %get-tuple-element.129, bf16[27,512,256]{2,1,0:T(8,128)(2,1)} %param.15), kind=kOutput, calls=%fused_computation.9 | convolution fusion | flops 271056896 | bytes 2359552 | tf_op jit(solution)/shard_map/fcp,co->fop/dot_general | solution.py:67
  84.8 1.6 %convolution_bitcast_fusion.2 = f32[4,256,256]{1,2,0:T(8,128)S(1)} fusion(bf16[4,512,15]{1,2,0:T(8,128)(2,1)S(1)} %get-tuple-element.56, bf16[4,512,241]{1,2,0:T(8,128)(2,1)S(1)} %get-tuple-element.50, pred[256]{0:T(512)(128)(4,1)S(1)} %get-tuple-element.126, bf16[27,512,256]{2,1,0:T(8,128)(2,1)} %param.15), kind=kOutput, calls=%fused_computation.6 | convolution fusion | flops 271056896 | bytes 2359552 | tf_op jit(solution)/shard_map/fcp,co->fop/dot_general | solution.py:67
  86.4 1.4 %convolution_bitcast_fusion.1 = f32[4,256,256]{1,2,0:T(8,128)S(1)} fusion(bf16[4,512,16]{1,2,0:T(8,128)(2,1)S(1)} %get-tuple-element.44, bf16[4,512,240]{1,2,0:T(8,128)(2,1)S(1)} %get-tuple-element.38, pred[256]{0:T(512)(128)(4,1)S(1)} %get-tuple-element.125, bf16[27,512,256]{2,1,0:T(8,128)(2,1)} %param.15), kind=kOutput, calls=%fused_computation.5 | convolution fusion | flops 271056896 | bytes 2359552 | tf_op jit(solution)/shard_map/fcp,co->fop/dot_general | solution.py:67
  87.8 1.6 %convolution_bitcast_fusion = f32[4,256,256]{1,2,0:T(8,128)S(1)} fusion(bf16[4,512,17]{1,2,0:T(8,128)(2,1)S(1)} %get-tuple-element.32, bf16[4,512,239]{1,2,0:T(8,128)(2,1)S(1)} %get-tuple-element.26, pred[256]{0:T(512)(128)(4,1)S(1)} %get-tuple-element.124, bf16[27,512,256]{2,1,0:T(8,128)(2,1)} %param.15), kind=kOutput, calls=%fused_computation.4 | convolution fusion | flops 271056896 | bytes 2359552 | tf_op jit(solution)/shard_map/fcp,co->fop/dot_general | solution.py:67
  89.4 1.5 %convolution_add_fusion.31 = f32[4,256,256]{2,1,0:T(8,128)S(1)} fusion(f32[4,256,256]{2,1,0:T(8,128)S(1)} %fusion.23, bf16[4,512,240]{1,2,0:T(8,128)(2,1)S(1)} %get-tuple-element.42, bf16[4,512,16]{1,2,0:T(8,128)(2,1)S(1)} %get-tuple-element.48, pred[256]{0:T(512)(128)(4,1)S(1)} %get-tuple-element.131, bf16[27,512,256]{2,1,0:T(8,128)(2,1)} %param.15), kind=kOutput, calls=%fused_computation.77 | convolution fusion | flops 271319040 | bytes 3408128 | tf_op jit(solution)/shard_map/fcp,co->fop/dot_general | solution.py:67
  100.8 2.5 %all-reduce.2 = (f32[16]{0:T(128)S(1)}, f32[16]{0:T(128)S(1)}) all-reduce(f32[16]{0:T(128)S(1)} %reduce_sum.75, f32[16]{0:T(128)S(1)} %reduce_sum.72), channel_id=1, replica_groups=mesh['groups'=2,'tile'=4,'chan'=2,'tm'=2] {'tm'}, use_global_device_ids=true, to_apply=%region_12.13 | all-reduce | flops 32 | bytes 256 | tf_op jit(solution)/shard_map/psum | solution.py:88
  104.5 8.5 %scatter_fusion.1 = f32[4,3,576]{1,0,2:T(4,128)S(1)} fusion(f32[4,3,576]{1,0,2:T(4,128)S(1)} %broadcast_in_dim.388, s32[256]{0:T(256)S(1)} %bitcast.321, f32[256,4,3]{2,1,0:T(4,128)S(1)} %copy.206), kind=kCustom, calls=%fused_computation.2 | custom fusion | flops 3072 | bytes 37888 | tf_op jit(solution)/shard_map/scatter-add | solution.py:102
  113.6 3.4 %collective-permute-start.5 = (f32[4,3,144]{2,0,1:T(4,128)S(1)}, f32[4,3,144]{2,0,1:T(4,128)S(1)}, u32[]{:S(2)}, u32[]{:S(2)}) collective-permute-start(f32[4,3,144]{2,0,1:T(4,128)S(1)} %get-tuple-element.112), channel_id=1, source_target_pairs={{0,4},{4,8},{8,12},{1,5},{5,9},{9,13},{2,6},{6,10},{10,14},{3,7},{... | collective-permute-start | bytes 20744 | tf_op jit(solution)/shard_map/ppermute | solution.py:36
  118.5 7.1 %psum.39 = f32[4,3,144]{2,0,1:T(4,128)S(1)} all-reduce(f32[4,3,144]{2,0,1:T(4,128)S(1)} %fusion.326), channel_id=1, replica_groups=mesh['groups'=2,'tile'=4,'chan'=2,'tm'=2] {'chan'}, use_global_device_ids=true, to_apply=%region_14.15 | all-reduce | flops 1728 | bytes 13824 | tf_op jit(solution)/shard_map/psum | solution.py:162
  (154 shorter events, 39.6 us)
Async XLA Ops:
  6.5 38.0 %copy-start = (f32[4,256]{1,0:T(4,128)S(1)}, f32[4,256]{1,0:T(4,128)}, u32[]{:S(2)}) copy-start(f32[4,256]{1,0:T(4,128)} %param.19) | copy-start | bytes 12292
  6.5 18.4 %copy-start.3 = (bf16[27,16,256]{2,1,0:T(8,128)(2,1)S(1)}, bf16[27,16,256]{2,1,0:T(8,128)(2,1)}, u32[]{:S(2)}) copy-start(bf16[27,16,256]{2,1,0:T(8,128)(2,1)} %param.12) | copy-start | bytes 663556
  6.5 64.2 %all-gather.2.cloned.1.call-start = ((), (), s32[]{:S(2)}) async-start(), calls=%async_computation | async-start | bytes 2359296 | tf_op jit(solution)/shard_map/all_gather | solution.py:155
  6.5 7.3 %collective-permute-start = (bf16[4,16,144]{2,1,0:T(8,128)(2,1)}, bf16[4,16,144]{2,1,0:T(8,128)(2,1)S(1)}, u32[]{:S(2)}, u32[]{:S(2)}) collective-permute-start(bf16[4,16,144]{2,1,0:T(8,128)(2,1)} %param.10), channel_id=1, source_target_pairs={{0,4},{4,8},{8,12},{12,0},{1,5},{5,9},{9,13},{13,1},{2,6},{6,10},{... | collective-permute-start | bytes 55304 | tf_op jit(solution)/shard_map/ppermute | solution.py:23
  9.6 6.2 %collective-permute-start.1 = (bf16[4,16,144]{2,1,0:T(8,128)(2,1)}, bf16[4,16,144]{2,1,0:T(8,128)(2,1)S(1)}, u32[]{:S(2)}, u32[]{:S(2)}) collective-permute-start(bf16[4,16,144]{2,1,0:T(8,128)(2,1)} %param.10), channel_id=1, source_target_pairs={{0,12},{4,0},{8,4},{12,8},{1,13},{5,1},{9,5},{13,9},{2,14},{6,2},{... | collective-permute-start | bytes 55304 | tf_op jit(solution)/shard_map/ppermute | solution.py:26
  13.8 5.7 %collective-permute-start.2 = (bf16[4,16,144]{2,1,0:T(8,128)(2,1)S(1)}, bf16[4,16,144]{2,1,0:T(8,128)(2,1)S(1)}, u32[]{:S(2)}, u32[]{:S(2)}) collective-permute-start(bf16[4,16,144]{2,1,0:T(8,128)(2,1)S(1)} %collective-permute-done), channel_id=1, source_target_pairs={{0,4},{4,8},{8,12},{12,0},{1,5},{5,9},{9,13},{13,1},{2,6},{6,10},{... | collective-permute-start | bytes 55304 | tf_op jit(solution)/shard_map/ppermute | solution.py:23
  22.7 2.1 %collective-permute-start.3 = (bf16[2,16,256]{2,1,0:T(8,128)(2,1)S(1)}, bf16[2,16,256]{2,1,0:T(8,128)(2,1)S(1)}, u32[]{:S(2)}, u32[]{:S(2)}) collective-permute-start(bf16[2,16,256]{2,1,0:T(8,128)(2,1)S(1)} %slice.742), channel_id=1, source_target_pairs={{0,1},{2,3},{4,5},{6,7},{8,9},{10,11},{12,13},{14,15},{16,17},{18,... | collective-permute-start | bytes 49160 | tf_op jit(solution)/shard_map/ppermute | solution.py:36
  35.7 4.1 %copy-start.4 = (f32[256]{0:T(256)S(1)}, f32[256]{0:T(256)}, u32[]{:S(2)}) copy-start(f32[256]{0:T(256)} %param.14) | copy-start | bytes 3076
  35.7 4.1 %copy-start.5 = (f32[256]{0:T(256)S(1)}, f32[256]{0:T(256)}, u32[]{:S(2)}) copy-start(f32[256]{0:T(256)} %param.13) | copy-start | bytes 3076
  40.2 3.4 %collective-permute-start.4 = (bf16[2,256,256]{1,2,0:T(8,128)(2,1)S(1)}, bf16[2,256,256]{1,2,0:T(8,128)(2,1)S(1)}, u32[]{:S(2)}, u32[]{:S(2)}) collective-permute-start(bf16[2,256,256]{1,2,0:T(8,128)(2,1)S(1)} %slice.825), channel_id=1, source_target_pairs={{0,1},{2,3},{4,5},{6,7},{8,9},{10,11},{12,13},{14,15},{16,17},{18,... | collective-permute-start | bytes 786440 | tf_op jit(solution)/shard_map/ppermute | solution.py:36
  47.0 70.7 %collective-permute-start.10 = (f32[144]{0:T(256)S(1)}, f32[144]{0:T(256)S(1)}, u32[]{:S(2)}, u32[]{:S(2)}) collective-permute-start(f32[144]{0:T(256)S(1)} %get-tuple-element.117), channel_id=1, source_target_pairs={} | collective-permute-start | bytes 1736 | tf_op jit(solution)/shard_map/ppermute | solution.py:36
  47.7 70.7 %collective-permute-start.8 = (f32[144]{0:T(256)S(1)}, f32[144]{0:T(256)S(1)}, u32[]{:S(2)}, u32[]{:S(2)}) collective-permute-start(f32[144]{0:T(256)S(1)} %get-tuple-element.115), channel_id=1, source_target_pairs={{0,4},{4,8},{8,12},{1,5},{5,9},{9,13},{2,6},{6,10},{10,14},{3,7},{... | collective-permute-start | bytes 1736 | tf_op jit(solution)/shard_map/ppermute | solution.py:36
  49.0 69.4 %collective-permute-start.9 = (f32[144]{0:T(256)S(1)}, f32[144]{0:T(256)S(1)}, u32[]{:S(2)}, u32[]{:S(2)}) collective-permute-start(f32[144]{0:T(256)S(1)} %get-tuple-element.116), channel_id=1, source_target_pairs={} | collective-permute-start | bytes 1736 | tf_op jit(solution)/shard_map/ppermute | solution.py:36
  70.8 4.4 %copy-start.2 = (bf16[6,512,256]{1,2,0:T(8,128)(2,1)S(1)}, bf16[6,512,256]{1,2,0:T(8,128)(2,1)}, u32[]{:S(2)}) copy-start(bf16[6,512,256]{1,2,0:T(8,128)(2,1)} %all-gather.2.cloned.1.call-done) | copy-start | bytes 4718596
  84.8 6.1 %slice-start = ((s8[7077888]{0:T(1024)(128)(4,1)}), s8[4194304]{0:T(1024)(128)(4,1)S(1)}, s32[]{:S(2)}) async-start(s8[7077888]{0:T(1024)(128)(4,1)} %bitcast.317), calls=%async_computation.1 | async-start | bytes 8388608
  87.8 3.1 %slice-start.1 = ((s8[7077888]{0:T(1024)(128)(4,1)}), s8[2883584]{0:T(1024)(128)(4,1)S(1)}, s32[]{:S(2)}) async-start(s8[7077888]{0:T(1024)(128)(4,1)} %bitcast.317), calls=%async_computation.2 | async-start | bytes 5767168
  99.8 3.8 %copy-start.6 = (bf16[3,256]{1,0:T(4,128)(2,1)S(1)}, bf16[3,256]{1,0:T(4,128)(2,1)}, u32[]{:S(2)}) copy-start(bf16[3,256]{1,0:T(4,128)(2,1)} %param.18) | copy-start | bytes 4612
  99.8 3.8 %copy-start.7 = (f32[256]{0:T(256)S(1)}, f32[256]{0:T(256)}, u32[]{:S(2)}) copy-start(f32[256]{0:T(256)} %param.17) | copy-start | bytes 3076
  99.8 3.8 %copy-start.8 = (f32[256]{0:T(256)S(1)}, f32[256]{0:T(256)}, u32[]{:S(2)}) copy-start(f32[256]{0:T(256)} %param.16) | copy-start | bytes 3076
  104.1 22.2 %copy-start.1 = (f32[4,256]{1,0:T(4,128)S(1)}, f32[4,256]{1,0:T(4,128)}, u32[]{:S(2)}) copy-start(f32[4,256]{1,0:T(4,128)} %param.19) | copy-start | bytes 12292
  113.6 4.8 %collective-permute-start.5 = (f32[4,3,144]{2,0,1:T(4,128)S(1)}, f32[4,3,144]{2,0,1:T(4,128)S(1)}, u32[]{:S(2)}, u32[]{:S(2)}) collective-permute-start(f32[4,3,144]{2,0,1:T(4,128)S(1)} %get-tuple-element.112), channel_id=1, source_target_pairs={{0,4},{4,8},{8,12},{1,5},{5,9},{9,13},{2,6},{6,10},{10,14},{3,7},{... | collective-permute-start | bytes 20744 | tf_op jit(solution)/shard_map/ppermute | solution.py:36
  117.0 1.4 %collective-permute-start.6 = (f32[4,3,144]{2,0,1:T(4,128)S(1)}, f32[4,3,144]{2,0,1:T(4,128)S(1)}, u32[]{:S(2)}, u32[]{:S(2)}) collective-permute-start(f32[4,3,144]{2,0,1:T(4,128)S(1)} %get-tuple-element.113), channel_id=1, source_target_pairs={} | collective-permute-start | bytes 20744 | tf_op jit(solution)/shard_map/ppermute | solution.py:36
  117.7 0.8 collective-permute-start.7
Sparse Core Ops, SparseCore 0:
  44.7 26.0 all-gather.1
